TPU v7x, 128 devices: a whole 4x4x4 slice. The times are simulated.
128 devices in a mesh: dp: 4 (over x), tensor: 4 (over z), opt: 8 (over y, core).
Axes of the slice: x: 4, y: 4, z: 4, core: 2. Of those that a mesh axis runs over, the one named last changes fastest.
Arguments:
- inputs: bfloat16 [4096, 4096], P(('dp', 'tensor', 'opt')), may hold values from -6 to 6
- cotangent: bfloat16 [4096, 4096], P(('dp', 'tensor', 'opt')), may hold values from -6 to 6
- w_gate: bfloat16 [14336, 4096], P(('tensor', 'opt')), may hold values from -0.09375 to 0.09375
- w_up: bfloat16 [14336, 4096], P(('tensor', 'opt')), may hold values from -0.09375 to 0.09375
- w_down: bfloat16 [14336, 4096], P(('tensor', 'opt')), may hold values from -0.046875 to 0.046875
- chosen: int32 [32, 128], P(('tensor', 'opt')), may hold values from 0 to 447, as said below
- live_rows: int32 [32], P(('tensor', 'opt')), may hold values from 32 to 128, as said below
- master: float32 [32, 128, 3, 4096], P(('tensor', 'opt'), None, None, 'dp'), may hold values from -0.3 to 0.3
- moment_one: float32 [32, 128, 3, 4096], P(('tensor', 'opt'), None, None, 'dp'), may hold values from -2 to 2
- moment_two: float32 [32, 128, 3, 4096], P(('tensor', 'opt'), None, None, 'dp'), may hold values from 0.05 to 0.5
Outputs:
- input_grad: bfloat16 [4096, 4096], P(('dp', 'tensor', 'opt'))
- new_master: float32 [32, 128, 3, 4096], P(('tensor', 'opt'), None, None, 'dp')
- new_moment_one: float32 [32, 128, 3, 4096], P(('tensor', 'opt'), None, None, 'dp')
- new_moment_two: float32 [32, 128, 3, 4096], P(('tensor', 'opt'), None, None, 'dp')
Inputs may be any that keep to these rules, and one draw needn't show every extreme that they name: `chosen`: within one shard the 128 entries are distinct hidden units of that shard. `live_rows`: some shard uses all 128 slots and some shard only 32.
All inputs are finite; a program needn't handle non-finite values.
Results may differ from a plain program's by a relative error of at most 0.023.
Values may be sent and summed in bfloat16 or wider, within the bound.
A program may use at most 192 MiB of HBM per device.

v0:
```python
import jax
import jax.numpy as jnp
from jax import lax
from jax.sharding import PartitionSpec as P


def local(
    inputs, cotangent, w_gate, w_up, w_down, chosen, live_rows, master, moment_one, moment_two
):
    full_in, full_cot = (
        lax.all_gather(inputs, ("tensor", "opt"), axis=0, tiled=True),
        lax.all_gather(cotangent, ("tensor", "opt"), axis=0, tiled=True),
    )
    by_feature = (((1,), (1,)), ((), ()))
    gate_val = lax.dot_general(full_in, w_gate, by_feature, preferred_element_type=jnp.float32)
    up_val = lax.dot_general(full_in, w_up, by_feature, preferred_element_type=jnp.float32)
    sig_gate = jax.nn.sigmoid(gate_val)
    activ = gate_val * sig_gate
    hidden = (activ * up_val).astype(jnp.bfloat16)
    hidden_grad = lax.dot_general(full_cot, w_down, by_feature, preferred_element_type=jnp.float32)
    gate_grad = (hidden_grad * up_val * sig_gate * (1.0 + gate_val * (1.0 - sig_gate))).astype(
        jnp.bfloat16
    )
    up_grad = (hidden_grad * activ).astype(jnp.bfloat16)
    input_grad = lax.psum_scatter(
        (
            jnp.dot(gate_grad, w_gate, preferred_element_type=jnp.float32)
            + jnp.dot(up_grad, w_up, preferred_element_type=jnp.float32)
        ).astype(jnp.bfloat16),
        ("tensor", "opt"),
        scatter_dimension=0,
        tiled=True,
    )
    slot_index = chosen[0]
    sel_gate = jnp.take(gate_grad, slot_index, axis=1)
    sel_up = jnp.take(up_grad, slot_index, axis=1)
    sel_hidden = jnp.take(hidden, slot_index, axis=1)
    by_token = (((0,), (0,)), ((), ()))
    total_tokens = full_in.shape[0] * lax.axis_size("dp")
    partial_rows = jnp.stack(
        [
            lax.dot_general(sel_gate, full_in, by_token, preferred_element_type=jnp.float32),
            lax.dot_general(sel_up, full_in, by_token, preferred_element_type=jnp.float32),
            lax.dot_general(sel_hidden, full_cot, by_token, preferred_element_type=jnp.float32),
        ],
        axis=1,
    )
    row_grad = lax.psum_scatter(
        partial_rows.astype(jnp.bfloat16), "dp", scatter_dimension=2, tiled=True
    ).astype(jnp.float32)
    row_grad = (row_grad * (1.0 / float(total_tokens) ** 0.5))[None]
    first = 0.9 * moment_one + 0.1 * row_grad
    second = 0.95 * moment_two + 0.05 * row_grad * row_grad
    corr_one = 1.0 - 0.9**10
    corr_two = 1.0 - 0.95**10
    update = 0.01 * (first / corr_one) / (jnp.sqrt(second / corr_two) + 1e-08)
    slot_count = chosen.shape[1]
    in_use = (jnp.arange(slot_count, dtype=jnp.int32)[None, :] < live_rows[:, None])[
        :, :, None, None
    ]
    new_master = jnp.where(in_use, master - update, master)
    new_moment_one = jnp.where(in_use, first, moment_one)
    new_moment_two = jnp.where(in_use, second, moment_two)
    return (input_grad, new_master, new_moment_one, new_moment_two)


def solution(mesh):
    placed = (
        P(("dp", "tensor", "opt"), None),
        P(("dp", "tensor", "opt"), None),
        P(("tensor", "opt"), None),
        P(("tensor", "opt"), None),
        P(("tensor", "opt"), None),
        P(("tensor", "opt"), None),
        P(("tensor", "opt")),
        P(("tensor", "opt"), None, None, "dp"),
        P(("tensor", "opt"), None, None, "dp"),
        P(("tensor", "opt"), None, None, "dp"),
    )
    return jax.shard_map(
        local,
        mesh=mesh,
        in_specs=placed,
        out_specs=(
            P(("dp", "tensor", "opt"), None),
            P(("tensor", "opt"), None, None, "dp"),
            P(("tensor", "opt"), None, None, "dp"),
            P(("tensor", "opt"), None, None, "dp"),
        ),
        check_vma=False,
    )
```

profile of v0, /device:TPU:0, one launch (start us, length us, event | category | flops | bytes accessed | tf_op | source)
XLA Modules:
  0.0 290.6 jit_solution(1457455061809009355)
XLA Ops:
  7.2 0.0 all-gather.3.cloned.1.call-start
  7.2 0.7 all-gather.3.cloned.1.call-update
  7.9 0.0 all-gather.5.cloned.1.call-start
  7.9 0.7 all-gather.5.cloned.1.call-update
  8.6 0.0 reduce-scatter.5.cloned.1.call-start
  8.7 0.7 compare_select_fusion
  9.4 0.7 compare_and_fusion
  10.0 55.8 %all-gather.3.cloned.1.call-done = bf16[1024,4096]{1,0:T(8,128)(2,1)} async-done(((bf16[32,4096]{1,0:T(8,128)(2,1)}), bf16[1024,4096]{1,0:T(8,128)(2,1)}) %all-gather.3.cloned.1.call-update) | async-done | bytes 8388624 | tf_op jit(solution)/shard_map/all_gather | solution.py:12
  65.8 9.7 %fusion.26 = f32[1024,448]{0,1:T(8,128)} fusion(bf16[1024,4096]{1,0:T(8,128)(2,1)} %all-gather.3.cloned.1.call-done, bf16[448,4096]{1,0:T(8,128)(2,1)} %param.16), kind=kOutput, calls=%fused_computation.46 | convolution fusion | flops 3758096384 | bytes 13893632 | tf_op jit(solution)/shard_map/dot_general | solution.py:20
  75.4 45.2 %all-gather.5.cloned.1.call-done = bf16[1024,4096]{1,0:T(8,128)(2,1)} async-done(((bf16[32,4096]{1,0:T(8,128)(2,1)}), bf16[1024,4096]{1,0:T(8,128)(2,1)}) %all-gather.5.cloned.1.call-update) | async-done | bytes 8388624 | tf_op jit(solution)/shard_map/all_gather | solution.py:11
  120.6 0.0 copy-start
  120.6 0.0 copy-start.3
  120.6 0.0 copy-start.5
  120.6 7.7 %fusion.27 = f32[1024,448]{0,1:T(8,128)S(1)} fusion(bf16[1024,4096]{1,0:T(8,128)(2,1)} %all-gather.5.cloned.1.call-done, bf16[448,4096]{1,0:T(8,128)(2,1)} %param.14), kind=kOutput, calls=%fused_computation.47 | convolution fusion | flops 3758096384 | bytes 13893632 | tf_op jit(solution)/shard_map/dot_general | solution.py:15
  128.3 0.0 copy-done
  128.3 0.2 copy-done.3
  128.5 0.5 copy-done.5
  129.0 4.7 %multiply_convert_fusion = (bf16[1024,448]{0,1:T(8,128)(2,1)S(1)}, bf16[1024,448]{0,1:T(8,128)(2,1)S(1)}, bf16[1024,448]{0,1:T(8,128)(2,1)S(1)}) fusion(f32[1024,448]{0,1:T(8,128)S(1)} %fusion.27, f32[1024,448]{0,1:T(8,128)S(1)} %copy-done.5, bf16[1024,4096]{1,0:T(8,128)(2,1)S(1)} %copy-done, bf16[448,4096]{1,0:T(8,128)(2,1)S(1)} %copy-done.3), kind=kOutput, calls=%fused_computation.15 | convolution fusion | flops 3764977664 | bytes 18481152 | tf_op jit(solution)/shard_map/dot_general | solution.py:16
  133.7 0.9 gather_fusion.2
  134.6 0.9 gather_fusion
  135.4 0.9 gather_fusion.1
  136.3 0.0 slice-start
  136.3 4.8 %fusion.2 = bf16[128,1,4096]{2,0,1:T(8,128)(2,1)S(1)} fusion(bf16[1024,4096]{1,0:T(8,128)(2,1)} %all-gather.3.cloned.1.call-done, bf16[128,1024]{1,0:T(8,128)(2,1)S(1)} %gather_fusion.2, pred[128]{0:T(512)(128)(4,1)S(1)} %compare_and_fusion), kind=kOutput, calls=%fused_computation.9 | convolution fusion | flops 1074397184 | bytes 9699456 | tf_op jit(solution)/shard_map/dot_general | solution.py:44
  141.1 0.0 slice-start.1
  141.1 4.9 %fusion.1 = bf16[128,1,4096]{2,0,1:T(8,128)(2,1)S(1)} fusion(bf16[1024,4096]{1,0:T(8,128)(2,1)} %all-gather.5.cloned.1.call-done, bf16[128,1024]{1,0:T(8,128)(2,1)S(1)} %gather_fusion.1, pred[128]{0:T(512)(128)(4,1)S(1)} %compare_and_fusion), kind=kOutput, calls=%fused_computation.8 | convolution fusion | flops 1074397184 | bytes 9699456 | tf_op jit(solution)/shard_map/dot_general | solution.py:43
  146.0 0.0 slice-done
  146.0 0.0 slice-done.1
  146.0 1.3 fusion
  147.4 2.1 pad_maximum_fusion
  149.4 0.0 reduce-scatter.5.cloned.1.call-update
  149.4 0.0 reduce-scatter.3.cloned.1.call-start
  149.5 0.0 copy-start.4
  149.5 10.8 %fusion.28 = f32[1024,4096]{1,0:T(8,128)} fusion(bf16[1024,448]{0,1:T(8,128)(2,1)S(1)} %get-tuple-element.6, bf16[448,4096]{1,0:T(8,128)(2,1)} %param.14), kind=kOutput, calls=%fused_computation.48 | convolution fusion | flops 3758096384 | bytes 21364736 | tf_op jit(solution)/shard_map/dot_general | solution.py:27
  160.3 0.0 copy-done.4
  160.3 10.4 %add_convert_fusion = bf16[1024,4096]{1,0:T(8,128)(2,1)} fusion(f32[1024,4096]{1,0:T(8,128)} %fusion.28, bf16[1024,448]{0,1:T(8,128)(2,1)S(1)} %get-tuple-element.7, bf16[448,4096]{1,0:T(8,128)(2,1)S(1)} %copy-done.4), kind=kOutput, calls=%fused_computation.3 | convolution fusion | flops 3766484992 | bytes 29753344 | tf_op jit(solution)/shard_map/dot_general | solution.py:28
  170.7 0.0 copy-start.1
  170.7 0.0 copy-start.2
  170.7 0.0 reduce-scatter.3.cloned.1.call-update
  171.5 15.8 %reduce-scatter.5.cloned.1.call-done = bf16[128,3,1024]{2,0,1:T(8,128)(2,1)} async-done(((bf16[128,3,4096]{2,0,1:T(8,128)(2,1)}), bf16[128,3,1024]{2,0,1:T(8,128)(2,1)}) %reduce-scatter.5.cloned.1.call-update) | async-done | bytes 786448 | tf_op jit(solution)/shard_map/reduce_scatter | solution.py:48
  187.3 0.0 copy-done.1
  187.3 0.0 copy-done.2
  187.3 5.5 %fusion.10 = (f32[1,128,3,1024]{3,1,2,0:T(8,128)}, f32[1,128,3,1024]{3,1,2,0:T(8,128)}, f32[1,128,3,1024]{3,1,2,0:T(8,128)}) fusion(f32[1,128,3,1024]{3,1,2,0:T(8,128)S(1)} %copy-done.1, bf16[128,3,1024]{2,0,1:T(8,128)(2,1)} %reduce-scatter.5.cloned.1.call-done, pred[128]{0:T(512)(128)(4,1)S(1)} %iota_compare_fusion, f32[1,128,3,1024]{3,1,2,0:T(8,128)S(1)} %copy-done.2, ...), kind=kLoop, calls=%fused_computation.26 | loop fusion | flops 6684672 | bytes 10223744 | tf_op jit(solution)/shard_map/jit(_where)/select_n | solution.py:63
  192.8 91.3 %reduce-scatter.3.cloned.1.call-done = bf16[32,4096]{1,0:T(8,128)(2,1)} async-done(((bf16[1024,4096]{1,0:T(8,128)(2,1)}), bf16[32,4096]{1,0:T(8,128)(2,1)}) %reduce-scatter.3.cloned.1.call-update) | async-done | bytes 262160 | tf_op jit(solution)/shard_map/reduce_scatter | solution.py:25
  (3 shorter events, 0.0 us)
Async XLA Ops:
  7.2 58.6 %all-gather.3.cloned.1.call-start = ((), (), s32[]{:S(2)}) async-start(), calls=%async_computation.2 | async-start | bytes 8650752 | tf_op jit(solution)/shard_map/all_gather | solution.py:12
  7.9 112.7 %all-gather.5.cloned.1.call-start = ((), (), s32[]{:S(2)}) async-start(), calls=%async_computation.3 | async-start | bytes 8650752 | tf_op jit(solution)/shard_map/all_gather | solution.py:11
  8.6 178.7 %reduce-scatter.5.cloned.1.call-start = ((), (), s32[]{:S(2)}) async-start(), calls=%async_computation.5 | async-start | bytes 3932160 | tf_op jit(solution)/shard_map/reduce_scatter | solution.py:48
  120.6 7.7 %copy-start = (bf16[1024,4096]{1,0:T(8,128)(2,1)S(1)}, bf16[1024,4096]{1,0:T(8,128)(2,1)}, u32[]{:S(2)}) copy-start(bf16[1024,4096]{1,0:T(8,128)(2,1)} %all-gather.5.cloned.1.call-done) | copy-start | bytes 25165828
  120.6 7.9 %copy-start.3 = (bf16[448,4096]{1,0:T(8,128)(2,1)S(1)}, bf16[448,4096]{1,0:T(8,128)(2,1)}, u32[]{:S(2)}) copy-start(bf16[448,4096]{1,0:T(8,128)(2,1)} %param.15) | copy-start | bytes 11010052
  120.6 8.4 %copy-start.5 = (f32[1024,448]{0,1:T(8,128)S(1)}, f32[1024,448]{0,1:T(8,128)}, u32[]{:S(2)}) copy-start(f32[1024,448]{0,1:T(8,128)} %fusion.26) | copy-start | bytes 5505028
  136.3 9.7 %slice-start = ((s8[8388608]{0:T(1024)(128)(4,1)}), s8[4194304]{0:T(1024)(128)(4,1)S(1)}, s32[]{:S(2)}) async-start(s8[8388608]{0:T(1024)(128)(4,1)} %bitcast.50), calls=%async_computation.6 | async-start | bytes 8388608
  141.1 4.9 %slice-start.1 = ((s8[8388608]{0:T(1024)(128)(4,1)}), s8[4194304]{0:T(1024)(128)(4,1)S(1)}, s32[]{:S(2)}) async-start(s8[8388608]{0:T(1024)(128)(4,1)} %bitcast.50), calls=%async_computation.7 | async-start | bytes 8388608
  149.4 134.6 %reduce-scatter.3.cloned.1.call-start = ((), (), s32[]{:S(2)}) async-start(), calls=%async_computation.4 | async-start | bytes 8650752 | tf_op jit(solution)/shard_map/reduce_scatter | solution.py:25
  149.5 10.8 %copy-start.4 = (bf16[448,4096]{1,0:T(8,128)(2,1)S(1)}, bf16[448,4096]{1,0:T(8,128)(2,1)}, u32[]{:S(2)}) copy-start(bf16[448,4096]{1,0:T(8,128)(2,1)} %param.15) | copy-start | bytes 11010052
  170.7 16.6 %copy-start.1 = (f32[1,128,3,1024]{3,1,2,0:T(8,128)S(1)}, f32[1,128,3,1024]{3,1,2,0:T(8,128)}, u32[]{:S(2)}) copy-start(f32[1,128,3,1024]{3,1,2,0:T(8,128)} %param.21) | copy-start | bytes 4718596
  170.7 16.6 %copy-start.2 = (f32[1,128,3,1024]{3,1,2,0:T(8,128)S(1)}, f32[1,128,3,1024]{3,1,2,0:T(8,128)}, u32[]{:S(2)}) copy-start(f32[1,128,3,1024]{3,1,2,0:T(8,128)} %param.19) | copy-start | bytes 4718596
Sparse Core Ops, SparseCore 0:
  10.3 55.4 all-gather.2
  68.0 52.5 all-gather.4
  149.6 37.7 reduce-scatter.4
  191.4 92.5 reduce-scatter.2
where the time goes:
time: 291 us
  waiting for transfers between devices  209 us (72%)
  matrix products  54.2 us (19%)
  between operations  14.7 us (5%)
  other arithmetic  8.85 us (3%)
  local copies, waits for them, and re-layouts  3.36 us (1%)
    reduce_scatter x1, waiting for transfers between devices, local(): lax.psum_scatter((jnp.dot(gate_grad, w_gate, preferred_element_type=jnp.f...  91.3 us
    all_gather x1, waiting for transfers between devices, local(): lax.all_gather(cotangent, ('tensor', 'opt'), axis=0, tiled=True)  55.8 us
    all_gather x1, waiting for transfers between devices, local(): lax.all_gather(inputs, ('tensor', 'opt'), axis=0, tiled=True)  45.2 us
    reduce_scatter x1, waiting for transfers between devices, local(): lax.psum_scatter(partial_rows.astype(jnp.bfloat16), 'dp', scatter_dimensi...  15.8 us
    dot_general x1, matrix products, local(): jnp.dot(gate_grad, w_gate, preferred_element_type=jnp.float32)  10.8 us
    dot_general x1, matrix products, local(): jnp.dot(up_grad, w_up, preferred_element_type=jnp.float32)  10.4 us
    dot_general x1, matrix products, local(): lax.dot_general(full_cot, w_down, by_feature, preferred_element_type=jnp....  9.66 us
    dot_general x1, matrix products, local(): lax.dot_general(full_in, w_gate, by_feature, preferred_element_type=jnp.f...  7.65 us
  transfers between devices with their start and end apart: 4, of which 4 were waited for; matrix products, arithmetic and copies ran while one was open for 13% of the time, Pallas kernels for 0%

commit v1 on v0

v1 whole, which is shorter than its diff:
```python
import functools

import jax
import jax.numpy as jnp
from jax import lax
from jax.experimental import pallas as pl
from jax.experimental.pallas import tpu as pltpu
from jax.sharding import PartitionSpec as P

MESH = pl.DeviceIdType.MESH
F32, BF16 = jnp.float32, jnp.bfloat16
NT = (((1,), (1,)), ((), ()))
CHUNK = 1024
TILE = 256


class Messages:
    def __init__(self, send, recv):
        self.send, self.recv, self.all = send, recv, []

    def go(self, src, dst, device):
        i = len(self.all)
        copy = pltpu.make_async_remote_copy(
            src_ref=src,
            dst_ref=dst,
            send_sem=self.send.at[i],
            recv_sem=self.recv.at[i],
            device_id=device,
            device_id_type=MESH,
        )
        copy.start()
        self.all.append(copy)
        return copy


def kernel(
    inputs, cot, w_gate, w_up, w_down, chosen,
    grad_out, rows_out,
    xc, wg, wu, wd, wgs, wus, own_g, own_u, put_g, put_u, got_g, got_u,
    racc, xs1, xs2p, xs2m, xr1p, xr1m, xr2p, xr2m,
    psum, r11p, r11m, r12p, r12m, r21p, r21m, r22p, r22m,
    lsem, send, recv,
):
    dp, tz, op = lax.axis_index("dp"), lax.axis_index("tensor"), lax.axis_index("opt")
    y, core = op // 2, op % 2
    hidden_units = wg.shape[0]
    slots = racc.shape[1]
    width = wg.shape[1]
    quarter = width // 4

    def up(i):
        return (i + 1) % 4

    def down(i):
        return (i + 3) % 4

    xp, xm = (up(dp), tz, op), (down(dp), tz, op)
    yp, ym = (dp, tz, up(y) * 2 + core), (dp, tz, down(y) * 2 + core)
    zp, zm = (dp, up(tz), op), (dp, down(tz), op)
    sib = (dp, tz, y * 2 + 1 - core)
    first = ((yp, ym), (zp, zm))
    second = ((zp, zm), (yp, ym))

    local = []

    def bring(src, dst):
        copy = pltpu.make_async_copy(src, dst, lsem.at[len(local)])
        copy.start()
        local.append(copy)
        return copy

    mine = []
    for half in range(2):
        for kind, ref in enumerate((inputs, cot)):
            mine.append(bring(ref.at[pl.ds(half * 16, 16)], xc.at[kind, 0, half, 0, 0]))
    weights = [bring(w_gate, wg), bring(w_up, wu), bring(w_down, wd)]

    barrier = pltpu.get_barrier_semaphore()
    for peer in (xp, xm, yp, ym, zp, zm, sib):
        pl.semaphore_signal(barrier, inc=1, device_id=peer, device_id_type=MESH)
    pl.semaphore_wait(barrier, 7)
    for copy in mine:
        copy.wait()

    net = Messages(send, recv)

    def ahead(half, k2, k1):
        return xc.at[:, k2, half, k1, 0]

    one_p, one_m, two_in, two_cot = {}, {}, {}, {}
    far_p, far_m, far_in, far_cot = {}, {}, {}, {}
    shared = {}

    def share(half, k2, k1):
        shared[half, k2, k1] = net.go(ahead(half, k2, k1), xc.at[:, k2, half, k1, 1], sib)

    def across(half, k1):
        here = ahead(half, 0, k1)
        far_p[half, k1] = net.go(here, ahead(half, 3, k1), second[half][0])
        far_m[half, k1] = net.go(here, ahead(half, 1, k1), second[half][1])

    for half in range(2):
        here = ahead(half, 0, 0)
        one_p[half] = net.go(here, ahead(half, 0, 3), first[half][0])
        one_m[half] = net.go(here, ahead(half, 0, 1), first[half][1])
    for half in range(2):
        across(half, 0)
        share(half, 0, 0)
    for half in range(2):
        one_p[half].wait_recv()
        two_in[half] = net.go(xc.at[0, 0, half, 3, 0], xc.at[0, 0, half, 2, 0], first[half][0])
        one_m[half].wait_recv()
        two_cot[half] = net.go(xc.at[1, 0, half, 1, 0], xc.at[1, 0, half, 2, 0], first[half][1])
    for half in range(2):
        for k1 in (3, 1):
            across(half, k1)
            share(half, 0, k1)
    for half in range(2):
        two_in[half].wait_recv()
        two_cot[half].wait_recv()
        across(half, 2)
        share(half, 0, 2)
    sib_gate = net.go(w_gate, wgs, sib)
    sib_up = net.go(w_up, wus, sib)

    unit = lax.broadcasted_iota(jnp.int32, (slots, hidden_units), 1)
    pick = (unit == chosen[...]).astype(F32).astype(BF16)
    passed = {}

    def block(k2):
        for half in range(2):
            for k1 in range(4):
                shared[half, k2, k1].wait_recv()
        tokens = 2 * 4 * 2 * 16
        x = xc[0, k2].reshape(tokens, width)
        c = xc[1, k2].reshape(tokens, width)
        gate = lax.dot_general(x, wg[...], NT, preferred_element_type=F32)
        upv = lax.dot_general(x, wu[...], NT, preferred_element_type=F32)
        back = lax.dot_general(c, wd[...], NT, preferred_element_type=F32)
        sig = jax.nn.sigmoid(gate)
        activ = gate * sig
        hid = (activ * upv).astype(BF16)
        gg = (back * upv * sig * (1.0 + gate * (1.0 - sig))).astype(BF16)
        ug = (back * activ).astype(BF16)
        for value, own, put in ((gg, own_g, put_g), (ug, own_u, put_u)):
            split = value.reshape(8, 2, 16, hidden_units)
            own[k2] = split[:, 0].reshape(128, hidden_units)
            put[k2] = split[:, 1].reshape(128, hidden_units)
        passed[k2] = (net.go(put_g.at[k2], got_g.at[k2], sib), net.go(put_u.at[k2], got_u.at[k2], sib))
        for kind, (value, rows) in enumerate(((gg, x), (ug, x), (hid, c))):
            sel = lax.dot_general(pick, value, NT, preferred_element_type=F32).astype(BF16)
            part = jnp.dot(sel, rows, preferred_element_type=F32)
            if k2 == 0:
                racc[kind] = part
            else:
                racc[kind] += part

    for copy in weights:
        copy.wait()
    block(0)

    for k1 in (0, 3, 1, 2):
        for half in range(2):
            far_p[half, k1].wait_recv()
            far_in[half, k1] = net.go(xc.at[0, 3, half, k1, 0], xc.at[0, 2, half, k1, 0], second[half][0])
            share(half, 3, k1)
            far_m[half, k1].wait_recv()
            far_cot[half, k1] = net.go(xc.at[1, 1, half, k1, 0], xc.at[1, 2, half, k1, 0], second[half][1])
            share(half, 1, k1)

    def last(k1):
        for half in range(2):
            far_in[half, k1].wait_recv()
            far_cot[half, k1].wait_recv()
            share(half, 2, k1)

    block(3)
    last(0)
    last(3)
    block(1)
    last(1)
    last(2)
    block(2)

    def part_of(k):
        return pl.ds(pl.multiple_of(((dp + k) % 4) * quarter, quarter), quarter)

    lo, hi = slice(0, slots // 2), slice(slots // 2, slots)
    xs1[...] = racc[:, :, part_of(2)].astype(BF16)
    x1p = net.go(xs1.at[:, lo], xr1p, xp)
    x1m = net.go(xs1.at[:, hi], xr1m, xm)

    sib_gate.wait_recv()
    sib_up.wait_recv()
    for pair in passed.values():
        for copy in pair:
            copy.wait_recv()

    def chunk_sums(j):
        def tile(i, carry):
            at = pl.ds(pl.multiple_of(j * CHUNK + i * TILE, TILE), TILE)
            total = jnp.zeros((512, TILE), F32)
            for grads, weight in ((own_g, wg), (own_u, wu), (got_g, wgs), (got_u, wus)):
                total += jnp.dot(
                    grads[...].reshape(512, hidden_units), weight[:, at], preferred_element_type=F32
                )
            psum[:, :, :, :, at] = total.astype(BF16).reshape(4, 2, 4, 16, TILE)
            return carry

        lax.fori_loop(0, CHUNK // TILE, tile, 0)

    flows = [{} for _ in range(width // CHUNK)]

    def add(*parts):
        total = parts[0].astype(F32)
        for part in parts[1:]:
            total += part.astype(F32)
        return total.astype(BF16)

    def spans(j):
        mid = CHUNK // 2
        whole = pl.ds(j * CHUNK, CHUNK)
        return whole, pl.ds(j * CHUNK, mid), pl.ds(j * CHUNK + mid, mid), pl.ds(j * mid, mid)

    def stage0(j):
        chunk_sums(j)
        whole, a, b, s = spans(j)
        for half in range(2):
            flows[j][0, half] = (
                net.go(psum.at[2, half, :, :, a], r11p.at[half, :, :, s], second[half][0]),
                net.go(psum.at[2, half, :, :, b], r11m.at[half, :, :, s], second[half][1]),
            )

    def stage1(j):
        whole, a, b, s = spans(j)
        for half in range(2):
            p, m = flows[j][0, half]
            p.wait_recv()
            psum[1, half, :, :, a] = add(psum[1, half, :, :, a], r11p[half, :, :, s])
            fp = net.go(psum.at[1, half, :, :, whole], r12p.at[half, :, :, whole], second[half][0])
            m.wait_recv()
            psum[3, half, :, :, b] = add(psum[3, half, :, :, b], r11m[half, :, :, s])
            fm = net.go(psum.at[3, half, :, :, whole], r12m.at[half, :, :, whole], second[half][1])
            flows[j][1, half] = (fp, fm)

    def stage2(j):
        whole, a, b, s = spans(j)
        for half in range(2):
            for copy in flows[j][1, half]:
                copy.wait_recv()
            psum[0, half, :, :, whole] = add(
                psum[0, half, :, :, whole], r12p[half, :, :, whole], r12m[half, :, :, whole]
            )
            flows[j][2, half] = (
                net.go(psum.at[0, half, 2, :, a], r21p.at[half, :, s], first[half][0]),
                net.go(psum.at[0, half, 2, :, b], r21m.at[half, :, s], first[half][1]),
            )

    def stage3(j):
        whole, a, b, s = spans(j)
        for half in range(2):
            p, m = flows[j][2, half]
            p.wait_recv()
            psum[0, half, 1, :, a] = add(psum[0, half, 1, :, a], r21p[half, :, s])
            fp = net.go(psum.at[0, half, 1, :, whole], r22p.at[half, :, whole], first[half][0])
            m.wait_recv()
            psum[0, half, 3, :, b] = add(psum[0, half, 3, :, b], r21m[half, :, s])
            fm = net.go(psum.at[0, half, 3, :, whole], r22m.at[half, :, whole], first[half][1])
            flows[j][3, half] = (fp, fm)

    def stage4(j):
        whole, a, b, s = spans(j)
        for half in range(2):
            for copy in flows[j][3, half]:
                copy.wait_recv()
            grad_out[half * 16 : half * 16 + 16, whole] = add(
                psum[0, half, 0, :, whole], r22p[half, :, whole], r22m[half, :, whole]
            )

    x2 = []

    def x_middle():
        x1p.wait_recv()
        value = racc[:, :, part_of(1)]
        xs2p[:, hi] = value[:, hi].astype(BF16)
        xs2p[:, lo] = (value[:, lo] + xr1p[...].astype(F32)).astype(BF16)
        x2.append(net.go(xs2p, xr2p, xp))
        x1m.wait_recv()
        value = racc[:, :, part_of(3)]
        xs2m[:, lo] = value[:, lo].astype(BF16)
        xs2m[:, hi] = (value[:, hi] + xr1m[...].astype(F32)).astype(BF16)
        x2.append(net.go(xs2m, xr2m, xm))

    stages = (stage0, stage1, stage2, stage3, stage4)
    n = len(flows)
    for step in range(n + len(stages) - 1):
        for s, stage in enumerate(stages):
            if 0 <= step - s < n:
                stage(step - s)
        if step == 2:
            x_middle()
    for copy in x2:
        copy.wait_recv()
    rows_out[...] = (
        racc[:, :, part_of(0)] + xr2p[...].astype(F32) + xr2m[...].astype(F32)
    ).astype(rows_out.dtype)
    for copy in net.all:
        copy.wait_send()


def exchange(inputs, cotangent, w_gate, w_up, w_down, chosen, slots):
    units, width = w_gate.shape
    grads = (4, 128, units)
    quarter = (3, slots, width // 4)
    half_quarter = (3, slots // 2, width // 4)
    any_space = pl.BlockSpec(memory_space=pl.ANY)
    vmem = pl.BlockSpec(memory_space=pltpu.VMEM)
    messages = 72 + 2 + 8 + 4 + 16 * (width // CHUNK)
    return pl.pallas_call(
        kernel,
        out_shape=(
            jax.ShapeDtypeStruct((32, width), BF16),
            jax.ShapeDtypeStruct(quarter, BF16),
        ),
        in_specs=[any_space] * 5 + [vmem],
        out_specs=(vmem, vmem),
        scratch_shapes=[
            pltpu.VMEM((2, 4, 2, 4, 2, 16, width), BF16),
            pltpu.VMEM((units, width), BF16),
            pltpu.VMEM((units, width), BF16),
            pltpu.VMEM((units, width), BF16),
            pltpu.VMEM((units, width), BF16),
            pltpu.VMEM((units, width), BF16),
            pltpu.VMEM(grads, BF16),
            pltpu.VMEM(grads, BF16),
            pltpu.VMEM(grads, BF16),
            pltpu.VMEM(grads, BF16),
            pltpu.VMEM(grads, BF16),
            pltpu.VMEM(grads, BF16),
            pltpu.VMEM((3, slots, width), F32),
            pltpu.VMEM(quarter, BF16),
            pltpu.VMEM(quarter, BF16),
            pltpu.VMEM(quarter, BF16),
            pltpu.VMEM(half_quarter, BF16),
            pltpu.VMEM(half_quarter, BF16),
            pltpu.VMEM(quarter, BF16),
            pltpu.VMEM(quarter, BF16),
            pltpu.VMEM((4, 2, 4, 16, width), BF16),
            pltpu.VMEM((2, 4, 16, width // 2), BF16),
            pltpu.VMEM((2, 4, 16, width // 2), BF16),
            pltpu.VMEM((2, 4, 16, width), BF16),
            pltpu.VMEM((2, 4, 16, width), BF16),
            pltpu.VMEM((2, 16, width // 2), BF16),
            pltpu.VMEM((2, 16, width // 2), BF16),
            pltpu.VMEM((2, 16, width), BF16),
            pltpu.VMEM((2, 16, width), BF16),
            pltpu.SemaphoreType.DMA((7,)),
            pltpu.SemaphoreType.DMA((messages,)),
            pltpu.SemaphoreType.DMA((messages,)),
        ],
        compiler_params=pltpu.CompilerParams(
            collective_id=0, has_side_effects=True, vmem_limit_bytes=64 * 1024 * 1024 - 64 * 1024
        ),
    )(inputs, cotangent, w_gate, w_up, w_down, chosen)


def local(
    inputs, cotangent, w_gate, w_up, w_down, chosen, live_rows, master, moment_one, moment_two
):
    slots = chosen.shape[1]
    input_grad, row_grad = exchange(
        inputs, cotangent, w_gate, w_up, w_down, chosen.reshape(slots, 1), slots
    )
    total_tokens = inputs.shape[0] * 128
    row_grad = jnp.transpose(row_grad, (1, 0, 2)).astype(F32)
    row_grad = (row_grad * (1.0 / float(total_tokens) ** 0.5))[None]
    first = 0.9 * moment_one + 0.1 * row_grad
    second = 0.95 * moment_two + 0.05 * row_grad * row_grad
    corr_one = 1.0 - 0.9**10
    corr_two = 1.0 - 0.95**10
    update = 0.01 * (first / corr_one) / (jnp.sqrt(second / corr_two) + 1e-08)
    in_use = (jnp.arange(slots, dtype=jnp.int32)[None, :] < live_rows[:, None])[:, :, None, None]
    return (
        input_grad,
        jnp.where(in_use, master - update, master),
        jnp.where(in_use, first, moment_one),
        jnp.where(in_use, second, moment_two),
    )


def solution(mesh):
    token = P(("dp", "tensor", "opt"), None)
    hidden = P(("tensor", "opt"), None)
    state = P(("tensor", "opt"), None, None, "dp")
    return jax.shard_map(
        local,
        mesh=mesh,
        in_specs=(
            token, token, hidden, hidden, hidden, hidden, P(("tensor", "opt")), state, state, state,
        ),
        out_specs=(token, state, state, state),
        check_vma=False,
    )
```

time: 291 us -> 110 us (0.38)
  waiting for transfers between devices: 209 us -> 0 us
  Pallas kernels: 0 us -> 99.1 us
  matrix products: 54.2 us -> 0 us
  between operations: 14.7 us -> 1.3 us
    reduce_scatter x2 -> x0, waiting for transfers between devices: 107 us -> none  [the longest x1 91.3 us: local(): lax.psum_scatter((jnp.dot(gate_grad, w_gate, preferred_element_type=jnp.f...]
    all_gather x2 -> x0, waiting for transfers between devices: 101 us -> none  [the longest x1 55.8 us: local(): lax.all_gather(cotangent, ('tensor', 'opt'), axis=0, tiled=True)]
    pallas_call x0 -> x1, Pallas kernels: none -> 99.1 us  [exchange(): pl.pallas_call(kernel, out_shape=(jax.ShapeDtypeStruct((32, width), BF16)...]
    dot_general x8 -> x0, matrix products: 54.2 us -> none  [the longest x1 10.8 us: local(): jnp.dot(gate_grad, w_gate, preferred_element_type=jnp.float32)]
    select_n x2 -> x1, other arithmetic: 6.12 us -> 6.62 us  [local(): jnp.where(in_use, second, moment_two)]
  transfers between devices with their start and end apart: 4 -> 0, of which waited for: 4 -> 0; matrix products, arithmetic and copies ran while one was open for 13% -> 0% of each run, Pallas kernels for 0% -> 0%
where the time goes in v1:
time: 110 us
  Pallas kernels  99.1 us (90%)
  other arithmetic  7.2 us (7%)
  local copies, waits for them, and re-layouts  2.1 us (2%)
  between operations  1.3 us (1%)
    pallas_call x1, Pallas kernels, exchange(): pl.pallas_call(kernel, out_shape=(jax.ShapeDtypeStruct((32, width), BF16)...  99.1 us
    select_n x1, other arithmetic, local(): jnp.where(in_use, second, moment_two)  6.62 us

profile of v1, /device:TPU:0, one launch (start us, length us, event | category | flops | bytes accessed | tf_op | source)
XLA Modules:
  0.0 109.6 jit_solution(1697086649511231877)
XLA Ops:
  1.3 0.6 iota_compare_fusion
  1.9 1.4 %copy.14.chosen = s32[128,1]{1,0:T(8,128)} copy(s32[128,1]{0,1:T(1,128)} %bitcast.23) | data formatting | bytes 1024 | tf_op jit(solution)/shard_map/reshape | solution.py:372
  3.2 99.1 %shard_map.129 = (bf16[32,4096]{1,0:T(8,128)(2,1)}, bf16[3,128,1024]{2,1,0:T(8,128)(2,1)}) custom-call(bf16[32,4096]{1,0:T(8,128)(2,1)} %inputs.1, bf16[32,4096]{1,0:T(8,128)(2,1)} %cot.1, bf16[448,4096]{1,0:T(8,128)(2,1)} %w_gate.1, bf16[448,4096]{1,0:T(8,128)(2,1)} %w_up.1, bf16[448,4096]{1,0:T(8,128)(2,1)} %w_down.1, s32[128,1]{1,0:T(8,128)} %copy.14.chosen), custom_call_target="tpu_custom_call" | custom-call | tf_op jit(solution)/shard_map/pallas_call | solution.py:319
  102.3 0.0 copy-start
  102.3 6.6 %fusion.6 = (f32[1,128,3,1024]{3,1,2,0:T(8,128)}, f32[1,128,3,1024]{3,1,2,0:T(8,128)}, f32[1,128,3,1024]{3,1,2,0:T(8,128)}) fusion(f32[1,128,3,1024]{3,1,2,0:T(8,128)} %param.19, bf16[3,128,1024]{2,1,0:T(8,128)(2,1)} %get-tuple-element.7, pred[128]{0:T(512)(128)(4,1)} %iota_compare_fusion, f32[1,128,3,1024]{3,1,2,0:T(8,128)} %param.17, ...), kind=kLoop, calls=%fused_computation.10 | loop fusion | flops 6684672 | bytes 10223744 | tf_op jit(solution)/shard_map/jit(_where)/select_n | solution.py:387
  108.9 0.0 copy-done
  108.9 0.7 copy.17
Async XLA Ops:
  102.3 6.6 %copy-start = (bf16[32,4096]{1,0:T(8,128)(2,1)S(1)}, bf16[32,4096]{1,0:T(8,128)(2,1)}, u32[]{:S(2)}) copy-start(bf16[32,4096]{1,0:T(8,128)(2,1)} %get-tuple-element.15) | copy-start | bytes 786436

commit v2 on v0

v2 whole, which is shorter than its diff:
```python
import jax
import jax.numpy as jnp
from jax import lax
from jax.experimental import pallas as pl
from jax.experimental.pallas import tpu as pltpu
from jax.sharding import PartitionSpec as P

MESH = pl.DeviceIdType.MESH
F32, BF16 = jnp.float32, jnp.bfloat16
NT = (((1,), (1,)), ((), ()))
CHUNK = 1024
TILE = 512
ORDER = (0, 1, 3, 2)
SENDS, RECEIVES = 16, 112
TOKENS = 4096
ADAM_COLUMNS = 1024


def kernel(
    inputs, cot, w_gate, w_up, w_down, chosen,
    grad_out, rows_out,
    xc, wg, wu, wd, wgs, wus, own_g, own_u, put_g, put_u, got_g, got_u,
    racc, xs1, xs2p, xs2m, xr1p, xr1m, xr2p, xr2m,
    r1p, r1m, r1f, r2p, r2m, r2f,
    rows_here, lsem, send, recv,
):
    dp, tz, op = lax.axis_index("dp"), lax.axis_index("tensor"), lax.axis_index("opt")
    y, core = op // 2, op % 2
    units, width = wg.shape
    slots = racc.shape[1]
    quarter = width // 4

    def on(i, k):
        return (i + k) % 4

    xp, xm = (on(dp, 1), tz, op), (on(dp, 3), tz, op)
    yp, ym, yf = ((dp, tz, on(y, k) * 2 + core) for k in (1, 3, 2))
    zp, zm, zf = ((dp, on(tz, k), op) for k in (1, 3, 2))
    sib = (dp, tz, y * 2 + 1 - core)
    first = ((yp, ym, yf), (zp, zm, zf))
    second = ((zp, zm, zf), (yp, ym, yf))

    psum = xc.at[0, :, :, :, 1]
    brought = []

    def bring(src, dst):
        copy = pltpu.make_async_copy(src, dst, lsem.at[len(brought)])
        copy.start()
        brought.append(copy)
        return copy

    mine = []
    for half in range(2):
        for kind, ref in enumerate((inputs, cot)):
            mine.append(bring(ref.at[pl.ds(half * 16, 16)], xc.at[kind, 0, half, 0, 0]))

    barrier = pltpu.get_barrier_semaphore()
    peers = (xp, xm, yp, ym, yf, zp, zm, zf, sib)
    for peer in peers:
        pl.semaphore_signal(barrier, inc=1, device_id=peer, device_id_type=MESH)
    pl.semaphore_wait(barrier, len(peers))

    groups, arrivals = [], []

    def group(total):
        groups.append((send.at[len(groups)], total))
        return groups[-1][0]

    def arrival():
        arrivals.append(None)
        return recv.at[len(arrivals) - 1]

    def copy_of(src, dst, s, r, device):
        return pltpu.make_async_remote_copy(
            src_ref=src, dst_ref=dst, send_sem=s, recv_sem=r, device_id=device, device_id_type=MESH
        )

    def go(src, dst, s, device, r=None):
        copy = copy_of(src, dst, s, arrival() if r is None else r, device)
        copy.start()
        return copy

    def all_of(dst, r):
        return copy_of(dst, dst, groups[0][0], r, sib)

    s_one = group(xc.at[0, 0, 0])
    s_two = group(xc.at[0, 0, 0, pl.ds(0, 2)])
    s_far = group(xc.at[:, 0])
    s_farther = group(xc.at[0, 0])
    s_share = group(xc.at[:, :, :, :, 0])
    s_wg, s_wu = group(wgs), group(wus)
    s_g, s_u = group(put_g), group(put_u)
    s_x1, s_x2p, s_x2m = group(xs1), group(xs2p), group(xs2m)
    s_near, s_last, s_row = group(psum.at[pl.ds(1, 2)]), group(psum.at[3]), group(psum.at[0, :, pl.ds(1, 3)])

    pieces = {
        "near": (slice(0, 1), slice(0, 4)),
        "mid0": (slice(1, 3), slice(0, 2)),
        "mid1": (slice(1, 3), slice(2, 4)),
        "last": (slice(3, 4), slice(0, 4)),
    }
    shared = {}
    for name in pieces:
        shared[name] = arrival()

    def ds(s):
        return pl.ds(s.start, s.stop - s.start)

    def piece_of(k2, k1):
        for name, (a, b) in pieces.items():
            if a.start <= k2 < a.stop and b.start <= k1 < b.stop:
                return name

    def slot(half, k2, k1):
        return xc.at[:, k2, half, k1, 0]

    def share(half, k2, k1):
        go(slot(half, k2, k1), xc.at[:, k2, half, k1, 1], s_share, sib, shared[piece_of(k2, k1)])

    one_p, one_m, two_in, two_cot = {}, {}, {}, {}
    far_p, far_m, far_in, far_cot = {}, {}, {}, {}

    def across(half, k1):
        here = slot(half, 0, k1)
        far_p[half, k1] = go(here, slot(half, 2, k1), s_far, second[half][0])
        far_m[half, k1] = go(here, slot(half, 1, k1), s_far, second[half][1])

    for half in range(2):
        for kind, ref in enumerate((inputs, cot)):
            here = ref.at[pl.ds(half * 16, 16)]
            one_p[half, kind] = go(here, xc.at[kind, 0, half, 2, 0], s_one, first[half][0])
            one_m[half, 1 - kind] = go(here, xc.at[kind, 0, half, 1, 0], s_one, first[half][1])
    for copy in mine:
        copy.wait()
    for half in range(2):
        across(half, 0)
    for half in range(2):
        share(half, 0, 0)
    sib_gate = go(w_gate, wgs, s_wg, sib)
    sib_up = go(w_up, wus, s_wu, sib)
    weights = [bring(w_gate, wg), bring(w_up, wu), bring(w_down, wd)]
    unit = lax.broadcasted_iota(jnp.int32, (512, slots), 0)
    pick = jnp.transpose((unit == chosen[...]).astype(F32))[:, :units].astype(BF16)
    for half in range(2):
        one_p[half, 0].wait_recv()
        two_in[half] = go(xc.at[0, 0, half, 2, 0], xc.at[0, 0, half, 3, 0], s_two, first[half][0])
        one_m[half, 0].wait_recv()
        two_cot[half] = go(xc.at[1, 0, half, 1, 0], xc.at[1, 0, half, 3, 0], s_two, first[half][1])
    for k1, side in ((1, one_m), (2, one_p)):
        for half in range(2):
            side[half, 1].wait_recv()
            across(half, k1)
            share(half, 0, k1)
    for half in range(2):
        two_in[half].wait_recv()
        two_cot[half].wait_recv()
        across(half, 3)
        share(half, 0, 3)

    sums = {"near": (arrival(), arrival()), "mid": (arrival(), arrival()), "last": (arrival(), arrival())}

    def part_of(k):
        return pl.ds(pl.multiple_of(on(dp, k) * quarter, quarter), quarter)

    lo, hi = slice(0, slots // 2), slice(slots // 2, slots)
    x1 = []

    def forward(name):
        a, b = pieces[name]
        na, nb = a.stop - a.start, b.stop - b.start
        tokens = na * 2 * nb * 2 * 16
        all_of(xc.at[:, ds(a), :, ds(b), 1], shared[name]).wait_recv()
        x = xc[0, a, :, b].reshape(tokens, width)
        c = xc[1, a, :, b].reshape(tokens, width)
        ends = sums[name.rstrip("01")]
        picked = [0.0, 0.0, 0.0]
        for u in (slice(0, 256), slice(256, units)):
            gate = lax.dot_general(x, wg[u], NT, preferred_element_type=F32)
            upv = lax.dot_general(x, wu[u], NT, preferred_element_type=F32)
            back = lax.dot_general(c, wd[u], NT, preferred_element_type=F32)
            sig = jax.nn.sigmoid(gate)
            activ = gate * sig
            hid = (activ * upv).astype(BF16)
            gg = (back * upv * sig * (1.0 + gate * (1.0 - sig))).astype(BF16)
            ug = (back * activ).astype(BF16)
            for value, own, put in ((gg, own_g, put_g), (ug, own_u, put_u)):
                split = value.reshape(na * 2 * nb, 2, 16, u.stop - u.start)
                own[a, :, b, :, u] = split[:, 0].reshape(na, 2, nb, 16, u.stop - u.start)
                put[a, :, b, :, u] = split[:, 1].reshape(na, 2, nb, 16, u.stop - u.start)
            for i, value in enumerate((gg, ug, hid)):
                picked[i] += lax.dot_general(pick[:, u], value, NT, preferred_element_type=F32)
        for put, got, s, r in ((put_g, got_g, s_g, ends[0]), (put_u, got_u, s_u, ends[1])):
            for k2 in range(a.start, a.stop):
                go(put.at[k2, :, ds(b)], got.at[k2, :, ds(b)], s, sib, r)
        picked = [value.astype(BF16) for value in picked]
        both = jnp.concatenate(picked[:2], axis=0)
        if name != "last":
            part = jnp.dot(both, x, preferred_element_type=F32).reshape(2, slots, width)
            down = jnp.dot(picked[2], c, preferred_element_type=F32)
            if name == "near":
                racc[0:2] = part
                racc[2] = down
            else:
                racc[0:2] += part
                racc[2] += down
            return
        for k in (2, 1, 3, 0):
            at = part_of(k)
            for kinds, rows, values in ((2, 0, both), (1, 1, picked[2])):
                rows = xc[rows, a, :, b, :, :, at].reshape(tokens, quarter)
                part = jnp.dot(values, rows, preferred_element_type=F32).reshape(kinds, slots, quarter)
                for i in range(kinds):
                    kind = i if kinds == 2 else 2
                    total = racc[kind, :, at] + part[i]
                    if k != 2:
                        racc[kind, :, at] = total
                        continue
                    xs1[kind] = total.astype(BF16)
                    x1.append(
                        (
                            go(xs1.at[kind, ds(lo)], xr1p.at[kind], s_x1, xp),
                            go(xs1.at[kind, ds(hi)], xr1m.at[kind], s_x1, xm),
                        )
                    )

    def sum_chip(a, start, stop):
        rows = (a.stop - a.start) * 128

        def tile(i, carry):
            at = pl.ds(pl.multiple_of(start + i * TILE, TILE), TILE)
            total = jnp.zeros((rows, TILE), F32)
            for grads, weight in ((own_g, wg), (own_u, wu), (got_g, wgs), (got_u, wus)):
                total += jnp.dot(grads[a].reshape(rows, units), weight[:, at], preferred_element_type=F32)
            psum[a, :, :, :, at] = total.astype(BF16).reshape(a.stop - a.start, 2, 4, 16, TILE)
            return carry

        lax.fori_loop(0, (stop - start) // TILE, tile, 0)

    def passed(name, a):
        for got, r in zip((got_g, got_u), sums[name]):
            all_of(got.at[ds(a)], r).wait_recv()

    def onward(k1):
        for half in range(2):
            far_p[half, k1].wait_recv()
            far_in[half, k1] = go(xc.at[0, 2, half, k1, 0], xc.at[0, 3, half, k1, 0], s_farther, second[half][0])
            share(half, 2, k1)
            far_m[half, k1].wait_recv()
            far_cot[half, k1] = go(xc.at[1, 1, half, k1, 0], xc.at[1, 3, half, k1, 0], s_farther, second[half][1])
            share(half, 1, k1)

    def landed(k1):
        for half in range(2):
            far_in[half, k1].wait_recv()
            far_cot[half, k1].wait_recv()
            share(half, 3, k1)

    near, mid, last = slice(0, 1), slice(1, 3), slice(3, 4)
    for copy in weights:
        copy.wait()
    forward("near")
    onward(0)
    passed("near", near)
    sib_gate.wait_recv()
    sib_up.wait_recv()
    sum_chip(near, 0, width)
    onward(1)
    forward("mid0")
    onward(2)
    onward(3)
    forward("mid1")
    landed(0)
    landed(1)
    passed("mid", mid)
    landed(2)
    sum_chip(mid, 0, width // 2)
    landed(3)
    sum_chip(mid, width // 2, width)
    flow = {}
    for half in range(2):
        flow["p", half] = go(psum.at[1, half], r1p.at[half], s_near, second[half][0])
        flow["m", half] = go(psum.at[2, half], r1m.at[half], s_near, second[half][1])
    forward("last")
    passed("last", last)
    n = width // CHUNK

    def span(j):
        return pl.ds(j * CHUNK, CHUNK)

    for j in range(n):
        sum_chip(last, j * CHUNK, (j + 1) * CHUNK)
        for half in range(2):
            flow["f", half, j] = go(
                psum.at[3, half, :, :, span(j)], r1f.at[half, :, :, span(j)], s_last, second[half][2]
            )

    x2 = []
    for kind in range(3):
        p, m = x1[kind]
        p.wait_recv()
        value = racc[kind, :, part_of(1)]
        xs2p[kind, hi] = value[hi].astype(BF16)
        xs2p[kind, lo] = (value[lo] + xr1p[kind].astype(F32)).astype(BF16)
        fp = go(xs2p.at[kind], xr2p.at[kind], s_x2p, xp)
        m.wait_recv()
        value = racc[kind, :, part_of(3)]
        xs2m[kind, lo] = value[lo].astype(BF16)
        xs2m[kind, hi] = (value[hi] + xr1m[kind].astype(F32)).astype(BF16)
        x2.append((fp, go(xs2m.at[kind], xr2m.at[kind], s_x2m, xm)))

    def add(*parts):
        total = parts[0].astype(F32)
        for part in parts[1:]:
            total += part.astype(F32)
        return total.astype(BF16)

    def second_sums(j):
        at = span(j)
        for half in range(2):
            if j == 0:
                flow["p", half].wait_recv()
                flow["m", half].wait_recv()
            flow["f", half, j].wait_recv()
            psum[0, half, :, :, at] = add(
                psum[0, half, :, :, at], r1p[half, :, :, at], r1m[half, :, :, at], r1f[half, :, :, at]
            )
            flow["r", half, j] = [
                go(psum.at[0, half, k1, :, at], dst.at[half, :, at], s_row, first[half][k])
                for k1, dst, k in ((3, r2f, 2), (1, r2p, 0), (2, r2m, 1))
            ]

    def first_sums(j):
        at = span(j)
        for half in range(2):
            for copy in flow["r", half, j]:
                copy.wait_recv()
            grad_out[half * 16 : half * 16 + 16, at] = add(
                psum[0, half, 0, :, at], r2p[half, :, at], r2m[half, :, at], r2f[half, :, at]
            )

    for j in range(n):
        second_sums(j)
        if j > 0:
            first_sums(j - 1)
    first_sums(n - 1)

    for kind in range(3):
        for copy in x2[kind]:
            copy.wait_recv()
        total = racc[kind, :, part_of(0)] + xr2p[kind].astype(F32) + xr2m[kind].astype(F32)
        rows_here[kind] = total.astype(BF16)
        bring(rows_here.at[kind], rows_out.at[kind])
    for copy in brought[-3:]:
        copy.wait()
    for s, total in groups:
        copy_of(total, total, s, recv.at[0], sib).wait_send()


def adam(live, rows, master, moment_one, moment_two, new_master, new_one, new_two):
    in_use = lax.broadcasted_iota(jnp.int32, rows.shape, 1) < live[0]
    row_grad = rows[...].astype(F32) * (1.0 / float(TOKENS) ** 0.5)
    m1, m2, weight = moment_one[...], moment_two[...], master[...]
    first = 0.9 * m1 + 0.1 * row_grad
    second = 0.95 * m2 + 0.05 * row_grad * row_grad
    step = first * (0.01 / (1.0 - 0.9**10)) / (jnp.sqrt(second * (1.0 / (1.0 - 0.95**10))) + 1e-08)
    new_master[...] = jnp.where(in_use, weight - step, weight)
    new_one[...] = jnp.where(in_use, first, m1)
    new_two[...] = jnp.where(in_use, second, m2)


def local(
    inputs, cotangent, w_gate, w_up, w_down, chosen, live_rows, master, moment_one, moment_two
):
    slots = chosen.shape[1]
    units, width = w_gate.shape
    grads = (4, 2, 4, 16, units)
    quarter = (3, slots, width // 4)
    half_quarter = (3, slots // 2, width // 4)
    any_space = pl.BlockSpec(memory_space=pl.ANY)
    vmem = pl.BlockSpec(memory_space=pltpu.VMEM)
    weight = pltpu.VMEM((units, width), BF16)
    state = tuple(jnp.transpose(a[0], (1, 0, 2)) for a in (master, moment_one, moment_two))
    wide = jax.ShapeDtypeStruct(quarter, F32)
    input_grad, row_grad = pl.pallas_call(
        kernel,
        out_shape=(jax.ShapeDtypeStruct((32, width), BF16), jax.ShapeDtypeStruct(quarter, BF16)),
        in_specs=[any_space] * 5 + [vmem],
        out_specs=(vmem, any_space),
        scratch_shapes=[
            pltpu.VMEM((2, 4, 2, 4, 2, 16, width), BF16),
            *[weight] * 5,
            *[pltpu.VMEM(grads, BF16)] * 6,
            pltpu.VMEM((3, slots, width), F32),
            *[pltpu.VMEM(quarter, BF16)] * 3,
            *[pltpu.VMEM(half_quarter, BF16)] * 2,
            *[pltpu.VMEM(quarter, BF16)] * 2,
            *[pltpu.VMEM((2, 4, 16, width), BF16)] * 3,
            *[pltpu.VMEM((2, 16, width), BF16)] * 3,
            pltpu.VMEM(quarter, BF16),
            pltpu.SemaphoreType.DMA((10,)),
            pltpu.SemaphoreType.DMA((SENDS,)),
            pltpu.SemaphoreType.DMA((RECEIVES,)),
        ],
        compiler_params=pltpu.CompilerParams(
            collective_id=0, has_side_effects=True, vmem_limit_bytes=58 * 1024 * 1024
        ),
    )(inputs, cotangent, w_gate, w_up, w_down, chosen)
    block = pl.BlockSpec((1, slots, ADAM_COLUMNS), lambda i, j: (i, 0, j))
    new = pl.pallas_call(
        adam,
        grid=(3, quarter[2] // ADAM_COLUMNS),
        compiler_params=pltpu.CompilerParams(vmem_limit_bytes=16 * 1024 * 1024),
        out_shape=(wide, wide, wide),
        in_specs=[pl.BlockSpec(memory_space=pltpu.SMEM)] + [block] * 4,
        out_specs=(block, block, block),
    )(live_rows, row_grad, *state)
    return (input_grad, *(jnp.transpose(a, (1, 0, 2))[None] for a in new))


def solution(mesh):
    token = P(("dp", "tensor", "opt"), None)
    hidden = P(("tensor", "opt"), None)
    state = P(("tensor", "opt"), None, None, "dp")
    return jax.shard_map(
        local,
        mesh=mesh,
        in_specs=(
            token, token, hidden, hidden, hidden, hidden, P(("tensor", "opt")), state, state, state,
        ),
        out_specs=(token, state, state, state),
        check_vma=False,
    )
```

time: 291 us -> 101 us (0.35)
  waiting for transfers between devices: 209 us -> 0 us
  Pallas kernels: 0 us -> 97.8 us
  matrix products: 54.2 us -> 0 us
  between operations: 14.7 us -> 1.35 us
  other arithmetic: 8.85 us -> 0 us
    reduce_scatter x2 -> x0, waiting for transfers between devices: 107 us -> none  [the longest x1 91.3 us: local(): lax.psum_scatter((jnp.dot(gate_grad, w_gate, preferred_element_type=jnp.f...]
    all_gather x2 -> x0, waiting for transfers between devices: 101 us -> none  [the longest x1 55.8 us: local(): lax.all_gather(cotangent, ('tensor', 'opt'), axis=0, tiled=True)]
    pallas_call x0 -> x2, Pallas kernels: none -> 97.8 us  [the longest x1 94.8 us: local(): pl.pallas_call(kernel, out_shape=(jax.ShapeDtypeStruct((32, width), BF16)...]
    dot_general x8 -> x0, matrix products: 54.2 us -> none  [the longest x1 10.8 us: local(): jnp.dot(gate_grad, w_gate, preferred_element_type=jnp.float32)]
    select_n x2 -> x0, other arithmetic: 6.12 us -> none  [the longest x1 5.46 us: local(): new_moment_two = jnp.where(in_use, second, moment_two)]
  transfers between devices with their start and end apart: 4 -> 0, of which waited for: 4 -> 0; matrix products, arithmetic and copies ran while one was open for 13% -> 0% of each run, Pallas kernels for 0% -> 0%
where the time goes in v2:
time: 101 us
  Pallas kernels  97.8 us (97%)
  local copies, waits for them, and re-layouts  1.85 us (2%)
  between operations  1.35 us (1%)
    pallas_call x1, Pallas kernels, local(): pl.pallas_call(kernel, out_shape=(jax.ShapeDtypeStruct((32, width), BF16)...  94.8 us
    pallas_call x1, Pallas kernels, local(): pl.pallas_call(adam, grid=(3, quarter[2] // ADAM_COLUMNS), compiler_param...  3 us

profile of v2, /device:TPU:0, one launch (start us, length us, event | category | flops | bytes accessed | tf_op | source)
XLA Modules:
  0.0 101.0 jit_solution(13103955111341714870)
XLA Ops:
  1.3 0.0 copy-start
  1.3 0.0 copy-start.1
  1.3 0.0 copy-start.2
  1.3 94.8 %shard_map.129 = (bf16[32,4096]{1,0:T(8,128)(2,1)}, bf16[3,128,1024]{2,1,0:T(8,128)(2,1)}) custom-call(bf16[32,4096]{1,0:T(8,128)(2,1)} %inputs.1, bf16[32,4096]{1,0:T(8,128)(2,1)} %cot.1, bf16[448,4096]{1,0:T(8,128)(2,1)} %w_gate.1, bf16[448,4096]{1,0:T(8,128)(2,1)} %w_up.1, bf16[448,4096]{1,0:T(8,128)(2,1)} %w_down.1, s32[1,128]{1,0:T(1,128)} %chosen.1), custom_call_target="tpu_custom_call" | custom-call | tf_op jit(solution)/shard_map/pallas_call | solution.py:384
  96.1 0.0 copy-done
  96.1 0.0 copy-done.1
  96.2 0.0 copy-done.2
  96.2 0.0 copy-start.3
  96.2 1.1 %copy-done.3 = bf16[3,128,1024]{2,1,0:T(8,128)(2,1)S(1)} copy-done((bf16[3,128,1024]{2,1,0:T(8,128)(2,1)S(1)}, bf16[3,128,1024]{2,1,0:T(8,128)(2,1)}, u32[]{:S(2)}) %copy-start.3) | copy-done | bytes 786456
  97.3 0.0 copy-start.4
  97.3 3.0 %shard_map.130 = (f32[3,128,1024]{2,1,0:T(8,128)}, f32[3,128,1024]{2,1,0:T(8,128)}, f32[3,128,1024]{2,1,0:T(8,128)}) custom-call(s32[1]{0:T(128)S(6)} %copy.15.live, bf16[3,128,1024]{2,1,0:T(8,128)(2,1)S(1)} %copy-done.3, f32[3,128,1024]{2,1,0:T(8,128)S(1)} %bitcast.18, f32[3,128,1024]{2,1,0:T(8,128)S(1)} %bitcast.19, f32[3,128,1024]{2,1,0:T(8,128)S(1)} %bitcast.20), custom_call_target="tpu_custom_call" | custom-call | tf_op jit(solution)/shard_map/pallas_call | solution.py:409
  100.3 0.0 copy-done.4
  100.3 0.7 copy.16
Async XLA Ops:
  1.3 94.9 %copy-start = (f32[1,128,3,1024]{3,1,2,0:T(8,128)S(1)}, f32[1,128,3,1024]{3,1,2,0:T(8,128)}, u32[]{:S(2)}) copy-start(f32[1,128,3,1024]{3,1,2,0:T(8,128)} %param.17) | copy-start | bytes 4718596
  1.3 94.9 %copy-start.1 = (f32[1,128,3,1024]{3,1,2,0:T(8,128)S(1)}, f32[1,128,3,1024]{3,1,2,0:T(8,128)}, u32[]{:S(2)}) copy-start(f32[1,128,3,1024]{3,1,2,0:T(8,128)} %param.18) | copy-start | bytes 4718596
  1.3 94.9 %copy-start.2 = (f32[1,128,3,1024]{3,1,2,0:T(8,128)S(1)}, f32[1,128,3,1024]{3,1,2,0:T(8,128)}, u32[]{:S(2)}) copy-start(f32[1,128,3,1024]{3,1,2,0:T(8,128)} %param.19) | copy-start | bytes 4718596
  96.2 1.1 %copy-start.3 = (bf16[3,128,1024]{2,1,0:T(8,128)(2,1)S(1)}, bf16[3,128,1024]{2,1,0:T(8,128)(2,1)}, u32[]{:S(2)}) copy-start(bf16[3,128,1024]{2,1,0:T(8,128)(2,1)} %get-tuple-element.10.rows) | copy-start | bytes 2359300
  97.3 3.0 %copy-start.4 = (bf16[32,4096]{1,0:T(8,128)(2,1)S(1)}, bf16[32,4096]{1,0:T(8,128)(2,1)}, u32[]{:S(2)}) copy-start(bf16[32,4096]{1,0:T(8,128)(2,1)} %get-tuple-element.18) | copy-start | bytes 786436

commit v3 on v2

--- a/solution.py
+++ b/solution.py
@@ -163,7 +163,13 @@
         return pl.ds(pl.multiple_of(on(dp, k) * quarter, quarter), quarter)
 
     lo, hi = slice(0, slots // 2), slice(slots // 2, slots)
-    x1 = []
+    x1, x2 = {}, {}
+
+    def x_first(kind):
+        x1[kind] = (
+            go(xs1.at[kind, ds(lo)], xr1p.at[kind], s_x1, xp),
+            go(xs1.at[kind, ds(hi)], xr1m.at[kind], s_x1, xm),
+        )
 
     def forward(name):
         a, b = pieces[name]
@@ -204,37 +210,34 @@
                 racc[0:2] += part
                 racc[2] += down
             return
-        for k in (2, 1, 3, 0):
-            at = part_of(k)
-            for kinds, rows, values in ((2, 0, both), (1, 1, picked[2])):
-                rows = xc[rows, a, :, b, :, :, at].reshape(tokens, quarter)
-                part = jnp.dot(values, rows, preferred_element_type=F32).reshape(kinds, slots, quarter)
-                for i in range(kinds):
-                    kind = i if kinds == 2 else 2
+        for kinds, source, values in (((2,), 1, picked[2]), ((0, 1), 0, both)):
+            for k in (2, 1, 3, 0):
+                at = part_of(k)
+                rows = xc[source, a, :, b, :, :, at].reshape(tokens, quarter)
+                part = jnp.dot(values, rows, preferred_element_type=F32).reshape(len(kinds), slots, quarter)
+                for i, kind in enumerate(kinds):
                     total = racc[kind, :, at] + part[i]
-                    if k != 2:
+                    if k == 2:
+                        xs1[kind] = total.astype(BF16)
+                    else:
                         racc[kind, :, at] = total
-                        continue
-                    xs1[kind] = total.astype(BF16)
-                    x1.append(
-                        (
-                            go(xs1.at[kind, ds(lo)], xr1p.at[kind], s_x1, xp),
-                            go(xs1.at[kind, ds(hi)], xr1m.at[kind], s_x1, xm),
-                        )
-                    )
+                if k == 2:
+                    x_first(kinds[0])
+        x_first(1)
 
     def sum_chip(a, start, stop):
         rows = (a.stop - a.start) * 128
+        size = TILE * 256 // rows
 
         def tile(i, carry):
-            at = pl.ds(pl.multiple_of(start + i * TILE, TILE), TILE)
-            total = jnp.zeros((rows, TILE), F32)
+            at = pl.ds(pl.multiple_of(start + i * size, size), size)
+            total = 0.0
             for grads, weight in ((own_g, wg), (own_u, wu), (got_g, wgs), (got_u, wus)):
                 total += jnp.dot(grads[a].reshape(rows, units), weight[:, at], preferred_element_type=F32)
-            psum[a, :, :, :, at] = total.astype(BF16).reshape(a.stop - a.start, 2, 4, 16, TILE)
+            psum[a, :, :, :, at] = total.astype(BF16).reshape(a.stop - a.start, 2, 4, 16, size)
             return carry
 
-        lax.fori_loop(0, (stop - start) // TILE, tile, 0)
+        lax.fori_loop(0, (stop - start) // size, tile, 0)
 
     def passed(name, a):
         for got, r in zip((got_g, got_u), sums[name]):
@@ -272,14 +275,22 @@
     landed(0)
     landed(1)
     passed("mid", mid)
+    flow = {}
+
+    def send_near(start, stop):
+        at = pl.ds(start, stop - start)
+        for half in range(2):
+            for side, (k2, dst) in enumerate(((1, r1p), (2, r1m))):
+                flow[side, half, start] = go(
+                    psum.at[k2, half, :, :, at], dst.at[half, :, :, at], s_near, second[half][side]
+                )
+
     landed(2)
+    landed(3)
     sum_chip(mid, 0, width // 2)
-    landed(3)
+    send_near(0, width // 2)
     sum_chip(mid, width // 2, width)
-    flow = {}
-    for half in range(2):
-        flow["p", half] = go(psum.at[1, half], r1p.at[half], s_near, second[half][0])
-        flow["m", half] = go(psum.at[2, half], r1m.at[half], s_near, second[half][1])
+    send_near(width // 2, width)
     forward("last")
     passed("last", last)
     n = width // CHUNK
@@ -287,15 +298,16 @@
     def span(j):
         return pl.ds(j * CHUNK, CHUNK)
 
-    for j in range(n):
+    def sum_last(j):
         sum_chip(last, j * CHUNK, (j + 1) * CHUNK)
+
+    def send_last(j):
         for half in range(2):
             flow["f", half, j] = go(
                 psum.at[3, half, :, :, span(j)], r1f.at[half, :, :, span(j)], s_last, second[half][2]
             )
 
-    x2 = []
-    for kind in range(3):
+    def x_second(kind):
         p, m = x1[kind]
         p.wait_recv()
         value = racc[kind, :, part_of(1)]
@@ -306,7 +318,7 @@
         value = racc[kind, :, part_of(3)]
         xs2m[kind, lo] = value[lo].astype(BF16)
         xs2m[kind, hi] = (value[hi] + xr1m[kind].astype(F32)).astype(BF16)
-        x2.append((fp, go(xs2m.at[kind], xr2m.at[kind], s_x2m, xm)))
+        x2[kind] = (fp, go(xs2m.at[kind], xr2m.at[kind], s_x2m, xm))
 
     def add(*parts):
         total = parts[0].astype(F32)
@@ -317,9 +329,9 @@
     def second_sums(j):
         at = span(j)
         for half in range(2):
-            if j == 0:
-                flow["p", half].wait_recv()
-                flow["m", half].wait_recv()
+            for side in range(2):
+                if (side, half, j * CHUNK) in flow:
+                    flow[side, half, j * CHUNK].wait_recv()
             flow["f", half, j].wait_recv()
             psum[0, half, :, :, at] = add(
                 psum[0, half, :, :, at], r1p[half, :, :, at], r1m[half, :, :, at], r1f[half, :, :, at]
@@ -338,13 +350,25 @@
                 psum[0, half, 0, :, at], r2p[half, :, at], r2m[half, :, at], r2f[half, :, at]
             )
 
+    sum_last(0)
+    send_last(0)
+    x_second(2)
+    sum_last(1)
+    send_last(1)
+    x_second(0)
+    sum_last(2)
+    x_second(1)
     for j in range(n):
         second_sums(j)
-        if j > 0:
-            first_sums(j - 1)
-    first_sums(n - 1)
-
-    for kind in range(3):
+        if j + 2 < n:
+            send_last(j + 2)
+        if j + 3 < n:
+            sum_last(j + 3)
+        if j > 1:
+            first_sums(j - 2)
+    for j in range(n - 2, n):
+        first_sums(j)
+    for kind in (2, 0, 1):
         for copy in x2[kind]:
             copy.wait_recv()
         total = racc[kind, :, part_of(0)] + xr2p[kind].astype(F32) + xr2m[kind].astype(F32)

time: 101 us -> 97.9 us (0.969)
  Pallas kernels: 97.8 us -> 94.5 us
    pallas_call x1, Pallas kernels: 94.8 us -> 91.6 us  [local(): pl.pallas_call(kernel, out_shape=(jax.ShapeDtypeStruct((32, width), BF16)...]
where the time goes in v3:
time: 97.9 us; the launch traced here: 97.7 us
  Pallas kernels  94.5 us (97%)
  local copies, waits for them, and re-layouts  1.85 us (2%)
  between operations  1.35 us (1%)
    pallas_call x1, Pallas kernels, local(): pl.pallas_call(kernel, out_shape=(jax.ShapeDtypeStruct((32, width), BF16)...  91.6 us
    pallas_call x1, Pallas kernels, local(): pl.pallas_call(adam, grid=(3, quarter[2] // ADAM_COLUMNS), compiler_param...  3 us

profile of v3, /device:TPU:0, one launch (start us, length us, event | category | flops | bytes accessed | tf_op | source)
XLA Modules:
  0.0 97.7 jit_solution(715808435015725606)
XLA Ops:
  1.3 0.0 copy-start
  1.3 0.0 copy-start.1
  1.3 0.0 copy-start.2
  1.3 91.6 %shard_map.129 = (bf16[32,4096]{1,0:T(8,128)(2,1)}, bf16[3,128,1024]{2,1,0:T(8,128)(2,1)}) custom-call(bf16[32,4096]{1,0:T(8,128)(2,1)} %inputs.1, bf16[32,4096]{1,0:T(8,128)(2,1)} %cot.1, bf16[448,4096]{1,0:T(8,128)(2,1)} %w_gate.1, bf16[448,4096]{1,0:T(8,128)(2,1)} %w_up.1, bf16[448,4096]{1,0:T(8,128)(2,1)} %w_down.1, s32[1,128]{1,0:T(1,128)} %chosen.1), custom_call_target="tpu_custom_call" | custom-call | tf_op jit(solution)/shard_map/pallas_call | solution.py:408
  92.9 0.0 copy-done
  92.9 0.0 copy-done.1
  92.9 0.0 copy-done.2
  92.9 0.0 copy-start.3
  92.9 1.1 %copy-done.3 = bf16[3,128,1024]{2,1,0:T(8,128)(2,1)S(1)} copy-done((bf16[3,128,1024]{2,1,0:T(8,128)(2,1)S(1)}, bf16[3,128,1024]{2,1,0:T(8,128)(2,1)}, u32[]{:S(2)}) %copy-start.3) | copy-done | bytes 786456
  94.0 0.0 copy-start.4
  94.0 3.0 %shard_map.130 = (f32[3,128,1024]{2,1,0:T(8,128)}, f32[3,128,1024]{2,1,0:T(8,128)}, f32[3,128,1024]{2,1,0:T(8,128)}) custom-call(s32[1]{0:T(128)S(6)} %copy.15.live, bf16[3,128,1024]{2,1,0:T(8,128)(2,1)S(1)} %copy-done.3, f32[3,128,1024]{2,1,0:T(8,128)S(1)} %bitcast.18, f32[3,128,1024]{2,1,0:T(8,128)S(1)} %bitcast.19, f32[3,128,1024]{2,1,0:T(8,128)S(1)} %bitcast.20), custom_call_target="tpu_custom_call" | custom-call | tf_op jit(solution)/shard_map/pallas_call | solution.py:433
  97.0 0.0 copy-done.4
  97.0 0.7 copy.16
Async XLA Ops:
  1.3 91.6 %copy-start = (f32[1,128,3,1024]{3,1,2,0:T(8,128)S(1)}, f32[1,128,3,1024]{3,1,2,0:T(8,128)}, u32[]{:S(2)}) copy-start(f32[1,128,3,1024]{3,1,2,0:T(8,128)} %param.17) | copy-start | bytes 4718596
  1.3 91.6 %copy-start.1 = (f32[1,128,3,1024]{3,1,2,0:T(8,128)S(1)}, f32[1,128,3,1024]{3,1,2,0:T(8,128)}, u32[]{:S(2)}) copy-start(f32[1,128,3,1024]{3,1,2,0:T(8,128)} %param.18) | copy-start | bytes 4718596
  1.3 91.6 %copy-start.2 = (f32[1,128,3,1024]{3,1,2,0:T(8,128)S(1)}, f32[1,128,3,1024]{3,1,2,0:T(8,128)}, u32[]{:S(2)}) copy-start(f32[1,128,3,1024]{3,1,2,0:T(8,128)} %param.19) | copy-start | bytes 4718596
  92.9 1.1 %copy-start.3 = (bf16[3,128,1024]{2,1,0:T(8,128)(2,1)S(1)}, bf16[3,128,1024]{2,1,0:T(8,128)(2,1)}, u32[]{:S(2)}) copy-start(bf16[3,128,1024]{2,1,0:T(8,128)(2,1)} %get-tuple-element.10.rows) | copy-start | bytes 2359300
  94.0 3.0 %copy-start.4 = (bf16[32,4096]{1,0:T(8,128)(2,1)S(1)}, bf16[32,4096]{1,0:T(8,128)(2,1)}, u32[]{:S(2)}) copy-start(bf16[32,4096]{1,0:T(8,128)(2,1)} %get-tuple-element.18) | copy-start | bytes 786436

commit v4 on v3

--- a/solution.py
+++ b/solution.py
@@ -380,9 +380,17 @@
         copy_of(total, total, s, recv.at[0], sib).wait_send()
 
 
-def adam(live, rows, master, moment_one, moment_two, new_master, new_one, new_two):
-    in_use = lax.broadcasted_iota(jnp.int32, rows.shape, 1) < live[0]
-    row_grad = rows[...].astype(F32) * (1.0 / float(TOKENS) ** 0.5)
+def adam(live, all_rows, master, moment_one, moment_two, new_master, new_one, new_two, rows, sems):
+    kind = pl.program_id(0)
+
+    @pl.when(kind == 0)
+    def _():
+        for i in range(3):
+            pltpu.make_async_copy(all_rows.at[i], rows.at[i], sems.at[i]).start()
+
+    pltpu.make_async_copy(all_rows.at[kind], rows.at[kind], sems.at[kind]).wait()
+    in_use = lax.broadcasted_iota(jnp.int32, master.shape, 1) < live[0]
+    row_grad = rows[pl.ds(kind, 1)].astype(F32) * (1.0 / float(TOKENS) ** 0.5)
     m1, m2, weight = moment_one[...], moment_two[...], master[...]
     first = 0.9 * m1 + 0.1 * row_grad
     second = 0.95 * m2 + 0.05 * row_grad * row_grad
@@ -435,8 +443,9 @@
         grid=(3, quarter[2] // ADAM_COLUMNS),
         compiler_params=pltpu.CompilerParams(vmem_limit_bytes=16 * 1024 * 1024),
         out_shape=(wide, wide, wide),
-        in_specs=[pl.BlockSpec(memory_space=pltpu.SMEM)] + [block] * 4,
+        in_specs=[pl.BlockSpec(memory_space=pltpu.SMEM), pl.BlockSpec(memory_space=pltpu.HBM)] + [block] * 3,
         out_specs=(block, block, block),
+        scratch_shapes=[pltpu.VMEM(quarter, BF16), pltpu.SemaphoreType.DMA((3,))],
     )(live_rows, row_grad, *state)
     return (input_grad, *(jnp.transpose(a, (1, 0, 2))[None] for a in new))
 

time: 97.9 us -> 98 us (level)
  no operation moved by 1% of the time
where the time goes in v4:
time: 98 us; the launch traced here: 97.8 us
  Pallas kernels  94.6 us (97%)
  local copies, waits for them, and re-layouts  1.85 us (2%)
  between operations  1.36 us (1%)
    pallas_call x1, Pallas kernels, local(): pl.pallas_call(kernel, out_shape=(jax.ShapeDtypeStruct((32, width), BF16)...  91.6 us
    pallas_call x1, Pallas kernels, local(): pl.pallas_call(adam, grid=(3, quarter[2] // ADAM_COLUMNS), compiler_param...  3.07 us

profile of v4, /device:TPU:0, one launch (start us, length us, event | category | flops | bytes accessed | tf_op | source)
XLA Modules:
  0.0 97.8 jit_solution(1934515926144062029)
XLA Ops:
  1.3 0.0 copy-start
  1.3 0.0 copy-start.1
  1.3 0.0 copy-start.2
  1.3 91.6 %shard_map.129 = (bf16[32,4096]{1,0:T(8,128)(2,1)}, bf16[3,128,1024]{2,1,0:T(8,128)(2,1)}) custom-call(bf16[32,4096]{1,0:T(8,128)(2,1)} %inputs.1, bf16[32,4096]{1,0:T(8,128)(2,1)} %cot.1, bf16[448,4096]{1,0:T(8,128)(2,1)} %w_gate.1, bf16[448,4096]{1,0:T(8,128)(2,1)} %w_up.1, bf16[448,4096]{1,0:T(8,128)(2,1)} %w_down.1, s32[1,128]{1,0:T(1,128)} %chosen.1), custom_call_target="tpu_custom_call" | custom-call | tf_op jit(solution)/shard_map/pallas_call | solution.py:416
  92.9 0.0 copy-done
  92.9 0.0 copy-done.1
  92.9 0.0 copy-done.2
  92.9 0.0 copy-start.3
  92.9 1.1 %copy-done.3 = bf16[3,128,1024]{2,1,0:T(8,128)(2,1)S(1)} copy-done((bf16[3,128,1024]{2,1,0:T(8,128)(2,1)S(1)}, bf16[3,128,1024]{2,1,0:T(8,128)(2,1)}, u32[]{:S(2)}) %copy-start.3) | copy-done | bytes 786456
  94.0 0.0 copy-start.4
  94.0 3.1 %shard_map.130 = (f32[3,128,1024]{2,1,0:T(8,128)}, f32[3,128,1024]{2,1,0:T(8,128)}, f32[3,128,1024]{2,1,0:T(8,128)}) custom-call(s32[1]{0:T(128)S(6)} %copy.15.live, bf16[3,128,1024]{2,1,0:T(8,128)(2,1)S(1)} %copy-done.3, f32[3,128,1024]{2,1,0:T(8,128)S(1)} %bitcast.18, f32[3,128,1024]{2,1,0:T(8,128)S(1)} %bitcast.19, f32[3,128,1024]{2,1,0:T(8,128)S(1)} %bitcast.20), custom_call_target="tpu_custom_call" | custom-call | tf_op jit(solution)/shard_map/pallas_call | solution.py:441
  97.1 0.0 copy-done.4
  97.1 0.7 copy.16
Async XLA Ops:
  1.3 91.6 %copy-start = (f32[1,128,3,1024]{3,1,2,0:T(8,128)S(1)}, f32[1,128,3,1024]{3,1,2,0:T(8,128)}, u32[]{:S(2)}) copy-start(f32[1,128,3,1024]{3,1,2,0:T(8,128)} %param.17) | copy-start | bytes 4718596
  1.3 91.6 %copy-start.1 = (f32[1,128,3,1024]{3,1,2,0:T(8,128)S(1)}, f32[1,128,3,1024]{3,1,2,0:T(8,128)}, u32[]{:S(2)}) copy-start(f32[1,128,3,1024]{3,1,2,0:T(8,128)} %param.18) | copy-start | bytes 4718596
  1.3 91.6 %copy-start.2 = (f32[1,128,3,1024]{3,1,2,0:T(8,128)S(1)}, f32[1,128,3,1024]{3,1,2,0:T(8,128)}, u32[]{:S(2)}) copy-start(f32[1,128,3,1024]{3,1,2,0:T(8,128)} %param.19) | copy-start | bytes 4718596
  92.9 1.1 %copy-start.3 = (bf16[3,128,1024]{2,1,0:T(8,128)(2,1)S(1)}, bf16[3,128,1024]{2,1,0:T(8,128)(2,1)}, u32[]{:S(2)}) copy-start(bf16[3,128,1024]{2,1,0:T(8,128)(2,1)} %get-tuple-element.10.all_rows) | copy-start | bytes 2359300
  94.0 3.1 %copy-start.4 = (bf16[32,4096]{1,0:T(8,128)(2,1)S(1)}, bf16[32,4096]{1,0:T(8,128)(2,1)}, u32[]{:S(2)}) copy-start(bf16[32,4096]{1,0:T(8,128)(2,1)} %get-tuple-element.18) | copy-start | bytes 786436
